TPU v7x, 32 devices: a whole 2x2x4 slice. The times are simulated.
32 devices in a mesh: dp: 8 (over y, x, core), code: 4 (over z).
Axes of the slice: x: 2, y: 2, z: 4, core: 2. Of those that a mesh axis runs over, the one named last changes fastest.
Arguments:
- temporal_out: bfloat16 [1024, 4096], P('dp'), may hold values from -6 to 6
- depth_in: bfloat16 [4, 4096, 1024], P('code', 'dp'), may hold values from -0.09375 to 0.09375
- embed: bfloat16 [4, 1024, 1024], P('code'), may hold values from -6 to 6
- depth_w1: bfloat16 [4, 1024, 2112], P('code', None, 'dp'), may hold values from -0.1875 to 0.1875
- depth_w2: bfloat16 [4, 1024, 2112], P('code', None, 'dp'), may hold values from -0.125 to 0.125
- audio_tokens: int32 [1024, 4], P(None, 'code'), may hold values from 0 to 1023
- barge_mask: int32 [1024], P('dp'), may hold values 0 or 1
- out_grad: bfloat16 [1024, 4, 1024], P('dp', 'code'), may hold values from -6 to 6
Outputs:
- temporal_grad: bfloat16 [1024, 4096], P('dp', 'code')
- depth_in_grad: bfloat16 [4, 4096, 1024], P('code', 'dp')
- embed_grad: bfloat16 [4, 1024, 1024], P('code', 'dp')
- w1_grad: bfloat16 [4, 1024, 2112], P('code', None, 'dp')
- w2_grad: bfloat16 [4, 1024, 2112], P('code', None, 'dp')
All inputs are finite; a program needn't handle non-finite values. No bound on the sum of `barge_mask` on one device may be relied on, other than what follows from the above.
Results may differ from a plain program's by a relative error of at most 0.02.
Values may be sent and summed in bfloat16 or wider, within the bound.
A program may use at most 128 MiB of HBM per device.

v0:
```python
import jax
import jax.numpy as jnp
from jax import lax
from jax.sharding import PartitionSpec as P

EPS = 1e-06


def shifted(block, axis, distance):
    devices = range(lax.axis_size(axis))
    route = [(i - distance, i) for i in devices if i - distance in devices]
    return lax.ppermute(block, axis, route)


def matmul(left, right):
    return jnp.dot(left, right, preferred_element_type=jnp.float32)


def contract_rows(left, right):
    return lax.dot_general(
        left, right, (((0,), (0,)), ((), ())), preferred_element_type=jnp.float32
    )


def contract_cols(left, right):
    return lax.dot_general(
        left, right, (((1,), (1,)), ((), ())), preferred_element_type=jnp.float32
    )


def silu_slope(values):
    sigma = jax.nn.sigmoid(values)
    return sigma * (1.0 + values * (1.0 - sigma))


def per_device(
    temporal_out, depth_in, embed, depth_w1, depth_w2, audio_tokens, barge_mask, out_grad
):
    dp_index = lax.axis_index("dp")
    n_code = lax.axis_size("code")
    n_dp = lax.axis_size("dp")
    own_rows = temporal_out.shape[0]
    projection = lax.all_gather(depth_in[0], "dp", axis=0, tiled=True)
    table = embed[0]
    token_all = audio_tokens[:, 0]
    token_own = lax.dynamic_slice_in_dim(token_all, dp_index * own_rows, own_rows, 0)
    depth_base = matmul(temporal_out, projection) + jnp.take(table, token_own, axis=0).astype(
        jnp.float32
    )
    width_depth = depth_base.shape[1]
    w_first, w_second = (
        lax.all_gather(depth_w1[0], "dp", axis=1, tiled=True),
        lax.all_gather(depth_w2[0], "dp", axis=1, tiled=True),
    )

    def depth_hidden(resid):
        scale = lax.rsqrt(jnp.mean(resid * resid, axis=-1, keepdims=True) + EPS)
        normed = (resid * scale).astype(jnp.bfloat16)
        pre_act = matmul(normed, w_first)
        active = jax.nn.silu(pre_act).astype(jnp.bfloat16)
        return (scale, normed, pre_act, active)

    def forward_turn(turn_index, incoming):
        resid = depth_base + incoming.astype(jnp.float32)
        scale, normed, pre_act, active = depth_hidden(resid)
        state = (resid + contract_cols(active, w_second)).astype(jnp.bfloat16)
        return shifted(state, "code", 1)

    start_state = jnp.zeros((own_rows, width_depth), jnp.bfloat16)
    incoming = lax.fori_loop(0, n_code - 1, forward_turn, start_state)
    resid = depth_base + incoming.astype(jnp.float32)
    scale, normed, pre_act, active = depth_hidden(resid)
    unit_rows = resid * scale
    derivative = silu_slope(pre_act)
    cotangent = out_grad[:, 0, :].astype(jnp.float32) * barge_mask.astype(jnp.float32)[:, None]

    def depth_back(from_next):
        state_slope = cotangent + from_next.astype(jnp.float32)
        slope_b = state_slope.astype(jnp.bfloat16)
        pre_slope = (matmul(slope_b, w_second) * derivative).astype(jnp.bfloat16)
        norm_slope = contract_cols(pre_slope, w_first)
        carried = (
            state_slope
            + scale
            * (norm_slope - unit_rows * jnp.mean(norm_slope * unit_rows, axis=-1, keepdims=True))
        ).astype(jnp.bfloat16)
        return (carried, slope_b, pre_slope)

    def backward_turn(turn_index, from_next):
        return shifted(depth_back(from_next)[0], "code", -1)

    from_next = lax.fori_loop(0, n_code - 1, backward_turn, start_state)
    carried, slope_b, pre_slope = depth_back(from_next)
    first_grad, second_grad = (
        lax.psum_scatter(
            contract_rows(normed, pre_slope).astype(jnp.bfloat16),
            "dp",
            scatter_dimension=1,
            tiled=True,
        ).astype(jnp.float32),
        lax.psum_scatter(
            contract_rows(slope_b, active).astype(jnp.bfloat16),
            "dp",
            scatter_dimension=1,
            tiled=True,
        ).astype(jnp.float32),
    )
    temporal_grad = lax.psum_scatter(
        contract_cols(carried, projection).astype(jnp.bfloat16),
        "code",
        scatter_dimension=1,
        tiled=True,
    )
    slope_all = lax.all_gather(carried, "dp", axis=0, tiled=True)
    columns = lax.all_to_all(temporal_out, "dp", split_axis=1, concat_axis=0, tiled=True)
    group_cols = columns.reshape(n_dp, own_rows, columns.shape[1])
    group_slopes = slope_all.reshape(n_dp, own_rows, width_depth)
    proj_parts = jnp.einsum(
        "gri,grj->gij", group_cols, group_slopes, preferred_element_type=jnp.float32
    ).astype(jnp.bfloat16)
    proj_grad = jnp.sum(proj_parts, axis=0, dtype=jnp.float32)
    vocab_local = table.shape[0] // n_dp
    vocab_ids = lax.broadcasted_iota(jnp.int32, (1, vocab_local), 1) + dp_index * vocab_local
    onehot = (
        (token_all[:, None] == vocab_ids).astype(jnp.bfloat16).reshape(n_dp, own_rows, vocab_local)
    )
    table_parts = jnp.einsum(
        "grv,grj->gvj", onehot, group_slopes, preferred_element_type=jnp.float32
    ).astype(jnp.bfloat16)
    table_grad = jnp.sum(table_parts, axis=0, dtype=jnp.float32)
    return (
        temporal_grad,
        proj_grad.astype(jnp.bfloat16)[None],
        table_grad.astype(jnp.bfloat16)[None],
        first_grad.astype(jnp.bfloat16)[None],
        second_grad.astype(jnp.bfloat16)[None],
    )


def solution(mesh):
    in_specs = (
        P("dp", None),
        P("code", "dp", None),
        P("code", None, None),
        P("code", None, "dp"),
        P("code", None, "dp"),
        P(None, "code"),
        P("dp"),
        P("dp", "code", None),
    )
    out_specs = (
        P("dp", "code"),
        P("code", "dp", None),
        P("code", "dp", None),
        P("code", None, "dp"),
        P("code", None, "dp"),
    )
    return jax.shard_map(
        per_device, mesh=mesh, in_specs=in_specs, out_specs=out_specs, check_vma=False
    )
```

profile of v0, /device:TPU:0, one launch (start us, length us, event | category | flops | bytes accessed | tf_op | source)
XLA Modules:
  0.0 454.5 jit_solution(8667353064678828686)
XLA Ops:
  7.2 0.7 all-gather.12.cloned.1.call-update
  7.9 0.0 all-gather.14.cloned.1.call-start
  8.0 0.7 all-gather.14.cloned.1.call-update
  8.7 0.7 all-gather.10.cloned.1.call-update
  9.4 0.0 all-gather.8.cloned.1.call-start
  9.6 0.9 gather_fusion
  10.4 0.1 convert_multiply_fusion
  10.5 39.2 %all-gather.12.cloned.1.call-done = bf16[1,1024,2112]{1,2,0:T(8,128)(2,1)} async-done(((bf16[1,1024,264]{1,2,0:T(8,128)(2,1)}), bf16[1,1024,2112]{1,2,0:T(8,128)(2,1)}) %all-gather.12.cloned.1.call-update) | async-done | bytes 4325392 | tf_op jit(solution)/shard_map/all_gather | solution.py:52
  49.8 6.4 %copy.23 = bf16[1024,2112]{1,0:T(8,128)(2,1)} copy(bf16[1024,2112]{0,1:T(8,128)(2,1)} %bitcast.72) | data formatting | bytes 8650752 | tf_op jit(solution)/shard_map/while | solution.py:70
  56.2 32.6 %all-gather.14.cloned.1.call-done = bf16[1,1024,2112]{1,2,0:T(8,128)(2,1)} async-done(((bf16[1,1024,264]{1,2,0:T(8,128)(2,1)}), bf16[1,1024,2112]{1,2,0:T(8,128)(2,1)}) %all-gather.14.cloned.1.call-update) | async-done | bytes 4325392 | tf_op jit(solution)/shard_map/all_gather | solution.py:53
  88.8 6.4 %copy.24 = bf16[1024,2112]{1,0:T(8,128)(2,1)} copy(bf16[1024,2112]{0,1:T(8,128)(2,1)} %bitcast.73) | data formatting | bytes 8650752 | tf_op jit(solution)/shard_map/while | solution.py:70
  95.2 49.8 %all-gather.10.cloned.1.call-done = bf16[1,4096,1024]{2,1,0:T(8,128)(2,1)} async-done(((bf16[1,512,1024]{2,1,0:T(8,128)(2,1)}), bf16[1,4096,1024]{2,1,0:T(8,128)(2,1)}) %all-gather.10.cloned.1.call-update) | async-done | bytes 8388624 | tf_op jit(solution)/shard_map/all_gather | solution.py:43
  145.0 5.0 %fusion.19 = f32[128,1024]{1,0:T(8,128)S(1)} fusion(bf16[128,4096]{1,0:T(8,128)(2,1)} %param.12, bf16[1,4096,1024]{2,1,0:T(8,128)(2,1)} %all-gather.10.cloned.1.call-done, bf16[128,1024]{1,0:T(8,128)(2,1)S(1)} %gather_fusion, pred[128]{0:T(512)(128)(4,1)S(1)} %get-tuple-element.136), kind=kOutput, calls=%fused_computation.31 | convolution fusion | flops 1074135040 | bytes 10223744 | tf_op jit(solution)/shard_map/dot_general | solution.py:16
  150.0 55.3 %while.20 = (s32[]{:T(128)}, bf16[128,1024]{1,0:T(8,128)(2,1)S(1)}, f32[128,1024]{1,0:T(8,128)S(1)}, bf16[1024,2112]{1,0:T(8,128)(2,1)}, bf16[1024,2112]{1,0:T(8,128)(2,1)}, /*index=5*/s32[]{:T(128)}) while((s32[]{:T(128)}, bf16[128,1024]{1,0:T(8,128)(2,1)S(1)}, f32[128,1024]{1,0:T(8,128)S(1)}, bf16[1024,2112]{1,0:T(8,128)(2,1)}, ...), condition=%wide.region_2.3_spmd, body=%wide.region_0.0_spmd.sunk | while | flops 1110220928 | bytes 11536493 | solution.py:70
  150.0 0.2 multiply_reduce_fusion.6
  150.2 8.9 %fusion.60 = bf16[128,1024]{1,0:T(8,128)(2,1)} fusion(bf16[1024,2112]{1,0:T(8,128)(2,1)} %get-tuple-element.246, bf16[1024,2112]{1,0:T(8,128)(2,1)} %get-tuple-element.245, f32[128,1024]{1,0:T(8,128)S(1)} %get-tuple-element.244, bf16[128,1024]{1,0:T(8,128)(2,1)S(1)} %get-tuple-element.237, f32[128]{0:T(128)S(1)} %add_rsqrt_fusion.3), kind=kOutput, calls=%fused_computation.2.clone.1 | convolution fusion | flops 1109696512 | bytes 9699840 | tf_op jit(solution)/shard_map/while/body/eval_jaxpr/dot_general | solution.py:26
  159.1 3.4 collective-permute-start
  162.5 6.3 %collective-permute-done = bf16[128,1024]{1,0:T(8,128)(2,1)S(1)} collective-permute-done((bf16[128,1024]{1,0:T(8,128)(2,1)}, bf16[128,1024]{1,0:T(8,128)(2,1)S(1)}, u32[]{:S(2)}, u32[]{:S(2)}) %collective-permute-start) | collective-permute-done | bytes 262176 | tf_op jit(solution)/shard_map/while/body/eval_jaxpr/ppermute | solution.py:12
  168.7 0.2 multiply_reduce_fusion.6
  168.9 8.9 %fusion.60 = bf16[128,1024]{1,0:T(8,128)(2,1)} fusion(bf16[1024,2112]{1,0:T(8,128)(2,1)} %get-tuple-element.246, bf16[1024,2112]{1,0:T(8,128)(2,1)} %get-tuple-element.245, f32[128,1024]{1,0:T(8,128)S(1)} %get-tuple-element.244, bf16[128,1024]{1,0:T(8,128)(2,1)S(1)} %get-tuple-element.237, f32[128]{0:T(128)S(1)} %add_rsqrt_fusion.3), kind=kOutput, calls=%fused_computation.2.clone.1 | convolution fusion | flops 1109696512 | bytes 9699840 | tf_op jit(solution)/shard_map/while/body/eval_jaxpr/dot_general | solution.py:26
  177.8 4.3 collective-permute-start
  182.0 5.4 %collective-permute-done = bf16[128,1024]{1,0:T(8,128)(2,1)S(1)} collective-permute-done((bf16[128,1024]{1,0:T(8,128)(2,1)}, bf16[128,1024]{1,0:T(8,128)(2,1)S(1)}, u32[]{:S(2)}, u32[]{:S(2)}) %collective-permute-start) | collective-permute-done | bytes 262176 | tf_op jit(solution)/shard_map/while/body/eval_jaxpr/ppermute | solution.py:12
  187.4 0.2 multiply_reduce_fusion.6
  187.6 8.9 %fusion.60 = bf16[128,1024]{1,0:T(8,128)(2,1)} fusion(bf16[1024,2112]{1,0:T(8,128)(2,1)} %get-tuple-element.246, bf16[1024,2112]{1,0:T(8,128)(2,1)} %get-tuple-element.245, f32[128,1024]{1,0:T(8,128)S(1)} %get-tuple-element.244, bf16[128,1024]{1,0:T(8,128)(2,1)S(1)} %get-tuple-element.237, f32[128]{0:T(128)S(1)} %add_rsqrt_fusion.3), kind=kOutput, calls=%fused_computation.2.clone.1 | convolution fusion | flops 1109696512 | bytes 9699840 | tf_op jit(solution)/shard_map/while/body/eval_jaxpr/dot_general | solution.py:26
  196.5 4.3 collective-permute-start
  200.8 4.5 %collective-permute-done = bf16[128,1024]{1,0:T(8,128)(2,1)S(1)} collective-permute-done((bf16[128,1024]{1,0:T(8,128)(2,1)}, bf16[128,1024]{1,0:T(8,128)(2,1)S(1)}, u32[]{:S(2)}, u32[]{:S(2)}) %collective-permute-start) | collective-permute-done | bytes 262176 | tf_op jit(solution)/shard_map/while/body/eval_jaxpr/ppermute | solution.py:12
  205.3 0.2 multiply_reduce_fusion.3
  205.5 0.6 copy-done.1
  206.1 1.1 fusion.25
  207.2 4.9 %add_multiply_fusion = (f32[128,2112]{0,1:T(8,128)}, f32[128,2112]{0,1:T(8,128)}) fusion(bf16[1,1024,2112]{1,2,0:T(8,128)(2,1)} %all-gather.12.cloned.1.call-done, f32[128,1024]{1,0:T(8,128)S(1)} %fusion.25), kind=kOutput, calls=%fused_computation.33 | convolution fusion | flops 555671552 | bytes 7012352 | tf_op jit(solution)/shard_map/dot_general | solution.py:16
  212.1 59.2 %while.21 = (s32[]{:T(128)}, bf16[128,1024]{1,0:T(8,128)(2,1)S(1)}, f32[128,1024]{1,0:T(8,128)S(1)}, f32[128,1]{0,1:T(1,128)S(1)}, bf16[1024,2112]{1,0:T(8,128)(...) while((s32[]{:T(128)}, bf16[128,1024]{1,0:T(8,128)(2,1)S(1)}, ...), condition=%wide.region_6.7_spmd, body=%wide.region_4.6_spmd.sunk | while | flops 1109409792 | bytes 14715525 | solution.py:92
  212.1 9.2 %multiply_reduce_fusion.7 = (f32[128]{0:T(128)S(1)}, f32[128,1024]{1,0:T(8,128)}) fusion(f32[128,1024]{1,0:T(8,128)S(1)} %get-tuple-element.273, bf16[1024,2112]{1,0:T(8,128)(2,1)} %get-tuple-element.272, f32[128,2112]{0,1:T(8,128)} %get-tuple-element.271, bf16[1024,2112]{1,0:T(8,128)(2,1)} %get-tuple-element.270, ...), kind=kOutput, calls=%fused_computation.16.clone.1 | convolution fusion | flops 1108492160 | bytes 11567616 | tf_op jit(solution)/shard_map/while/body/eval_jaxpr/dot_general | solution.py:26
  221.4 1.9 add_convert_fusion.3
  223.3 1.3 collective-permute-start.1
  224.6 7.5 %collective-permute-done.1 = bf16[128,1024]{1,0:T(8,128)(2,1)S(1)} collective-permute-done((bf16[128,1024]{1,0:T(8,128)(2,1)}, bf16[128,1024]{1,0:T(8,128)(2,1)S(1)}, u32[]{:S(2)}, u32[]{:S(2)}) %collective-permute-start.1) | collective-permute-done | bytes 262176 | tf_op jit(solution)/shard_map/while/body/eval_jaxpr/ppermute | solution.py:12
  232.1 9.2 %multiply_reduce_fusion.7 = (f32[128]{0:T(128)S(1)}, f32[128,1024]{1,0:T(8,128)}) fusion(f32[128,1024]{1,0:T(8,128)S(1)} %get-tuple-element.273, bf16[1024,2112]{1,0:T(8,128)(2,1)} %get-tuple-element.272, f32[128,2112]{0,1:T(8,128)} %get-tuple-element.271, bf16[1024,2112]{1,0:T(8,128)(2,1)} %get-tuple-element.270, ...), kind=kOutput, calls=%fused_computation.16.clone.1 | convolution fusion | flops 1108492160 | bytes 11567616 | tf_op jit(solution)/shard_map/while/body/eval_jaxpr/dot_general | solution.py:26
  241.4 1.9 add_convert_fusion.3
  243.3 1.3 collective-permute-start.1
  244.6 7.2 %collective-permute-done.1 = bf16[128,1024]{1,0:T(8,128)(2,1)S(1)} collective-permute-done((bf16[128,1024]{1,0:T(8,128)(2,1)}, bf16[128,1024]{1,0:T(8,128)(2,1)S(1)}, u32[]{:S(2)}, u32[]{:S(2)}) %collective-permute-start.1) | collective-permute-done | bytes 262176 | tf_op jit(solution)/shard_map/while/body/eval_jaxpr/ppermute | solution.py:12
  251.7 9.2 %multiply_reduce_fusion.7 = (f32[128]{0:T(128)S(1)}, f32[128,1024]{1,0:T(8,128)}) fusion(f32[128,1024]{1,0:T(8,128)S(1)} %get-tuple-element.273, bf16[1024,2112]{1,0:T(8,128)(2,1)} %get-tuple-element.272, f32[128,2112]{0,1:T(8,128)} %get-tuple-element.271, bf16[1024,2112]{1,0:T(8,128)(2,1)} %get-tuple-element.270, ...), kind=kOutput, calls=%fused_computation.16.clone.1 | convolution fusion | flops 1108492160 | bytes 11567616 | tf_op jit(solution)/shard_map/while/body/eval_jaxpr/dot_general | solution.py:26
  261.0 1.9 add_convert_fusion.3
  262.9 1.3 collective-permute-start.1
  264.2 7.2 %collective-permute-done.1 = bf16[128,1024]{1,0:T(8,128)(2,1)S(1)} collective-permute-done((bf16[128,1024]{1,0:T(8,128)(2,1)}, bf16[128,1024]{1,0:T(8,128)(2,1)S(1)}, u32[]{:S(2)}, u32[]{:S(2)}) %collective-permute-start.1) | collective-permute-done | bytes 262176 | tf_op jit(solution)/shard_map/while/body/eval_jaxpr/ppermute | solution.py:12
  271.4 4.0 fusion.18
  275.4 3.3 multiply_reduce_fusion.2
  278.8 1.0 add_convert_fusion.1
  279.8 0.0 reduce-scatter.4.cloned.1.call-start
  279.8 7.4 %fusion.15 = bf16[128,4096]{1,0:T(8,128)(2,1)} fusion(bf16[128,1024]{1,0:T(8,128)(2,1)} %add_convert_fusion.1, bf16[1,4096,1024]{2,1,0:T(8,128)(2,1)} %all-gather.10.cloned.1.call-done), kind=kOutput, calls=%fused_computation.27 | convolution fusion | flops 1074266112 | bytes 9699328 | tf_op jit(solution)/shard_map/dot_general | solution.py:26
  287.2 0.0 reduce-scatter.8.cloned.1.call-start
  287.3 4.6 %convolution_convert_fusion = bf16[1024,2112]{0,1:T(8,128)(2,1)} fusion(f32[128,2112]{0,1:T(8,128)} %get-tuple-element.143, bf16[128,1024]{1,0:T(8,128)(2,1)S(1)} %get-tuple-element.75, bf16[128,1,1024]{2,0,1:T(8,128)(2,1)S(1)} %copy-done.7, f32[128]{0:T(128)S(1)} %convert_element_type.84), kind=kOutput, calls=%fused_computation.25 | convolution fusion | flops 557817856 | bytes 5931520 | tf_op jit(solution)/shard_map/dot_general | solution.py:20
  291.9 0.0 reduce-scatter.6.cloned.1.call-start
  292.0 1.0 copy-done.4
  293.0 3.3 convolution_convert_fusion.1
  296.3 1.2 copy-done.2
  297.5 1.3 copy.27
  298.8 2.3 copy.28
  301.1 3.6 all-to-all-start
  304.7 15.3 %all-to-all-done = bf16[128,8,512]{2,0,1:T(8,128)(2,1)S(1)} async-done(((bf16[128,8,512]{2,0,1:T(8,128)(2,1)}), bf16[128,8,512]{2,0,1:T(8,128)(2,1)S(1)}, u32[]{:S(2)}, u32[]{:S(2)}) %all-to-all-start) | async-done | bytes 1048608 | tf_op jit(solution)/shard_map/all_to_all | solution.py:115
  320.0 5.2 %convert_reduce_fusion = bf16[1024,512]{1,0:T(8,128)(2,1)} fusion(bf16[8,128,1024]{2,1,0:T(8,128)(2,1)} %bitcast.75, bf16[128,8,512]{2,0,1:T(8,128)(2,1)S(1)} %all-to-all-done), kind=kOutput, calls=%fused_computation.24 | convolution fusion | flops 1081606144 | bytes 4194304 | tf_op jit(solution)/shard_map/gri,grj->gij/dot_general | solution.py:118
  325.2 2.3 copy.30
  327.4 3.1 convert_reduce_fusion.1
  330.6 6.8 %reduce-scatter.4.cloned.1.call-done = bf16[128,1024]{1,0:T(8,128)(2,1)} async-done(((bf16[128,4096]{1,0:T(8,128)(2,1)}), bf16[128,1024]{1,0:T(8,128)(2,1)}) %reduce-scatter.4.cloned.1.call-update) | async-done | bytes 262160 | tf_op jit(solution)/shard_map/reduce_scatter | solution.py:108
  337.3 54.3 %reduce-scatter.8.cloned.1.call-done = bf16[1024,264]{0,1:T(8,128)(2,1)} async-done(((bf16[1024,2112]{0,1:T(8,128)(2,1)}), bf16[1024,264]{0,1:T(8,128)(2,1)}) %reduce-scatter.8.cloned.1.call-update) | async-done | bytes 540688 | tf_op jit(solution)/shard_map/reduce_scatter | solution.py:101
  391.7 56.0 %reduce-scatter.6.cloned.1.call-done = bf16[1024,264]{0,1:T(8,128)(2,1)} async-done(((bf16[1024,2112]{0,1:T(8,128)(2,1)}), bf16[1024,264]{0,1:T(8,128)(2,1)}) %reduce-scatter.6.cloned.1.call-update) | async-done | bytes 540688 | tf_op jit(solution)/shard_map/reduce_scatter | solution.py:95
  (38 shorter events, 0.3 us)
Async XLA Ops:
  7.2 2.4 copy-start
  7.2 2.3 copy-start.9
  7.2 2.3 copy-start.8
  7.2 42.6 %all-gather.12.cloned.1.call-start = ((), (), s32[]{:S(2)}) async-start(), calls=%async_computation.9 | async-start | bytes 4866048 | tf_op jit(solution)/shard_map/all_gather | solution.py:52
  7.9 2.5 copy-start.5
  7.9 80.9 %all-gather.14.cloned.1.call-start = ((), (), s32[]{:S(2)}) async-start(), calls=%async_computation.10 | async-start | bytes 4866048 | tf_op jit(solution)/shard_map/all_gather | solution.py:53
  8.7 136.3 %all-gather.10.cloned.1.call-start = ((), (), s32[]{:S(2)}) async-start(), calls=%async_computation.8 | async-start | bytes 9437184 | tf_op jit(solution)/shard_map/all_gather | solution.py:43
  9.4 310.6 %all-gather.8.cloned.1.call-start = ((), (), s32[]{:S(2)}) async-start(), calls=%async_computation.5 | async-start | bytes 2359296 | tf_op jit(solution)/shard_map/all_gather | solution.py:114
  159.1 9.7 %collective-permute-start = (bf16[128,1024]{1,0:T(8,128)(2,1)}, bf16[128,1024]{1,0:T(8,128)(2,1)S(1)}, u32[]{:S(2)}, u32[]{:S(2)}) collective-permute-start(bf16[128,1024]{1,0:T(8,128)(2,1)} %fusion.60), channel_id=1, source_target_pairs={{0,1},{1,2},{2,3},{4,5},{5,6},{6,7},{8,9},{9,10},{10,11},{12,13},{... | collective-permute-start | bytes 786440 | tf_op jit(solution)/shard_map/while/body/eval_jaxpr/ppermute | solution.py:12
  177.8 9.7 %collective-permute-start = (bf16[128,1024]{1,0:T(8,128)(2,1)}, bf16[128,1024]{1,0:T(8,128)(2,1)S(1)}, u32[]{:S(2)}, u32[]{:S(2)}) collective-permute-start(bf16[128,1024]{1,0:T(8,128)(2,1)} %fusion.60), channel_id=1, source_target_pairs={{0,1},{1,2},{2,3},{4,5},{5,6},{6,7},{8,9},{9,10},{10,11},{12,13},{... | collective-permute-start | bytes 786440 | tf_op jit(solution)/shard_map/while/body/eval_jaxpr/ppermute | solution.py:12
  196.5 8.8 %collective-permute-start = (bf16[128,1024]{1,0:T(8,128)(2,1)}, bf16[128,1024]{1,0:T(8,128)(2,1)S(1)}, u32[]{:S(2)}, u32[]{:S(2)}) collective-permute-start(bf16[128,1024]{1,0:T(8,128)(2,1)} %fusion.60), channel_id=1, source_target_pairs={{0,1},{1,2},{2,3},{4,5},{5,6},{6,7},{8,9},{9,10},{10,11},{12,13},{... | collective-permute-start | bytes 786440 | tf_op jit(solution)/shard_map/while/body/eval_jaxpr/ppermute | solution.py:12
  205.3 0.8 copy-start.1
  223.3 8.8 %collective-permute-start.1 = (bf16[128,1024]{1,0:T(8,128)(2,1)}, bf16[128,1024]{1,0:T(8,128)(2,1)S(1)}, u32[]{:S(2)}, u32[]{:S(2)}) collective-permute-start(bf16[128,1024]{1,0:T(8,128)(2,1)} %add_convert_fusion.3), channel_id=1, source_target_pairs={{1,0},{2,1},{3,2},{5,4},{6,5},{7,6},{9,8},{10,9},{11,10},{13,12},{... | collective-permute-start | bytes 786440 | tf_op jit(solution)/shard_map/while/body/eval_jaxpr/ppermute | solution.py:12
  243.3 8.5 %collective-permute-start.1 = (bf16[128,1024]{1,0:T(8,128)(2,1)}, bf16[128,1024]{1,0:T(8,128)(2,1)S(1)}, u32[]{:S(2)}, u32[]{:S(2)}) collective-permute-start(bf16[128,1024]{1,0:T(8,128)(2,1)} %add_convert_fusion.3), channel_id=1, source_target_pairs={{1,0},{2,1},{3,2},{5,4},{6,5},{7,6},{9,8},{10,9},{11,10},{13,12},{... | collective-permute-start | bytes 786440 | tf_op jit(solution)/shard_map/while/body/eval_jaxpr/ppermute | solution.py:12
  262.9 8.5 %collective-permute-start.1 = (bf16[128,1024]{1,0:T(8,128)(2,1)}, bf16[128,1024]{1,0:T(8,128)(2,1)S(1)}, u32[]{:S(2)}, u32[]{:S(2)}) collective-permute-start(bf16[128,1024]{1,0:T(8,128)(2,1)} %add_convert_fusion.3), channel_id=1, source_target_pairs={{1,0},{2,1},{3,2},{5,4},{6,5},{7,6},{9,8},{10,9},{11,10},{13,12},{... | collective-permute-start | bytes 786440 | tf_op jit(solution)/shard_map/while/body/eval_jaxpr/ppermute | solution.py:12
  275.4 3.4 copy-start.3
  275.4 3.4 copy-start.6
  279.8 7.5 %copy-start.7 = (bf16[128,1,1024]{2,0,1:T(8,128)(2,1)S(1)}, bf16[128,1,1024]{2,0,1:T(8,128)(2,1)}, u32[]{:S(2)}) copy-start(bf16[128,1,1024]{2,0,1:T(8,128)(2,1)} %param.19) | copy-start | bytes 786436
  279.8 57.5 %reduce-scatter.4.cloned.1.call-start = ((), (), s32[]{:S(2)}) async-start(), calls=%async_computation.4 | async-start | bytes 1310720 | tf_op jit(solution)/shard_map/reduce_scatter | solution.py:108
  287.2 104.4 %reduce-scatter.8.cloned.1.call-start = ((), (), s32[]{:S(2)}) async-start(), calls=%async_computation.7 | async-start | bytes 4866048 | tf_op jit(solution)/shard_map/reduce_scatter | solution.py:101
  291.9 1.0 copy-start.4
  291.9 155.7 %reduce-scatter.6.cloned.1.call-start = ((), (), s32[]{:S(2)}) async-start(), calls=%async_computation.6 | async-start | bytes 4866048 | tf_op jit(solution)/shard_map/reduce_scatter | solution.py:95
  296.3 1.2 copy-start.2
  301.1 18.9 %all-to-all-start = ((bf16[128,8,512]{2,0,1:T(8,128)(2,1)}), bf16[128,8,512]{2,0,1:T(8,128)(2,1)S(1)}, u32[]{:S(2)}, u32[]{:S(2)}) async-start(bf16[128,8,512]{2,0,1:T(8,128)(2,1)} %copy.28), calls=%async_computation.1 | async-start | bytes 2097152 | tf_op jit(solution)/shard_map/all_to_all | solution.py:115
Sparse Core Ops, SparseCore 0:
  9.9 39.8 all-gather.11
  51.7 37.1 all-gather.13
  90.7 54.2 all-gather.9
  279.9 27.3 all-gather.7
  310.0 27.2 reduce-scatter.3
  341.2 50.4 reduce-scatter.7
  395.7 51.9 reduce-scatter.5
where the time goes:
time: 455 us; the launch traced here: 454 us
  waiting for transfers between devices  294 us (65%)
  matrix products  95.1 us (21%)
  local copies, waits for them, and re-layouts  22.4 us (5%)
  starting transfers between devices  19.6 us (4%)
  between operations  14.3 us (3%)
  other arithmetic  8.67 us (2%)
    dot_general x8, matrix products, contract_cols(): lax.dot_general(left, right, (((1,), (1,)), ((), ())), preferred_element_...  65 us
    reduce_scatter x1, waiting for transfers between devices, per_device(): lax.psum_scatter(contract_rows(normed, pre_slope).astype(jnp.bfloat16), '...  56 us
    reduce_scatter x1, waiting for transfers between devices, per_device(): lax.psum_scatter(contract_rows(slope_b, active).astype(jnp.bfloat16), 'dp...  54.3 us
    all_gather x1, waiting for transfers between devices, per_device(): projection = lax.all_gather(depth_in[0], 'dp', axis=0, tiled=True)  49.8 us
    all_gather x1, waiting for transfers between devices, per_device(): lax.all_gather(depth_w1[0], 'dp', axis=1, tiled=True)  39.2 us
    ppermute x6, waiting for transfers between devices, shifted(): return lax.ppermute(block, axis, route)  38.1 us
    all_gather x1, waiting for transfers between devices, per_device(): lax.all_gather(depth_w2[0], 'dp', axis=1, tiled=True)  32.6 us
    ppermute x6, starting transfers between devices, shifted(): return lax.ppermute(block, axis, route)  15.8 us
  transfers between devices with their start and end apart: 14, of which 13 were waited for; matrix products, arithmetic and copies ran while one was open for 10% of the time, Pallas kernels for 0%

commit v1 on v0

v1 whole, which is shorter than its diff:
```python
import functools

import jax
import jax.numpy as jnp
from jax import lax
from jax.experimental import pallas as pl
from jax.experimental.pallas import tpu as pltpu
from jax.sharding import PartitionSpec as P

EPS = 1e-06
MESH = pl.DeviceIdType.MESH
CHUNKS = 2
TILE = 512


def dot_nt(left, right):
    return lax.dot_general(
        left, right, (((1,), (1,)), ((), ())), preferred_element_type=jnp.float32
    )


def dot_nn(left, right):
    return jnp.dot(left, right, preferred_element_type=jnp.float32)


def chain_kernel(
    n_dp,
    n_code,
    temporal,
    embedded,
    cot_ref,
    proj_own,
    w1_own,
    w2_own,
    temporal_grad,
    cols_all,
    normed_all,
    slope_all,
    carry_all,
    act_all,
    pre_all,
    proj,
    w1,
    w2,
    base,
    acc,
    incoming,
    returning,
    state,
    carry_out,
    deriv,
    act_t,
    pre_t,
    scale_ref,
    term,
    term_in,
    ring_send,
    ring_recv,
    pass_send,
    pass_recv,
    own_sem,
    chain_send,
    chain_recv,
    ag_send,
    ag_recv,
    swap_send,
    swap_recv,
    term_send,
    term_recv,
):
    dp = lax.axis_index("dp")
    code = lax.axis_index("code")
    rows, width = base.shape
    hidden = w1.shape[0]
    pad = hidden // n_dp
    depth = proj_own.shape[0]
    half = width // 2
    step_rows = rows // CHUNKS
    chips = n_dp // 2
    core = lax.rem(dp, 2)
    chip = dp // 2
    partner = chip * 2 + 1 - core

    def ring_place(c):
        return jnp.where(lax.rem(c, 2) == 0, c // 2, chips - 1 - c // 2)

    def ring_chip(p):
        p = lax.rem(p + 2 * chips, chips)
        return jnp.where(p < chips // 2, 2 * p, 2 * (chips - 1 - p) + 1)

    place = ring_place(chip)
    right = ring_chip(place + 1) * 2 + core
    left = ring_chip(place - 1) * 2 + core

    barrier = pltpu.get_barrier_semaphore()
    for other in range(1, n_dp):
        pl.semaphore_signal(
            barrier, inc=1, device_id=(lax.rem(dp + other, n_dp), code), device_id_type=MESH
        )
    for other in range(1, n_code):
        pl.semaphore_signal(
            barrier, inc=1, device_id=(dp, lax.rem(code + other, n_code)), device_id_type=MESH
        )
    pl.semaphore_wait(barrier, n_dp + n_code - 2)

    whole = (
        (proj_own, proj, depth),
        (w1_own, w1, pad),
        (w2_own, w2, pad),
    )

    def part(array, size, owner, way):
        start = pl.multiple_of(owner * size, 16)
        return array.at[pl.ds(start, size), pl.ds(way * half, half)]

    def ring_copy(i, way, step):
        own, full, size = whole[i]
        origin = ring_chip(place - step if way == 0 else place + step) * 2 + core
        dst = part(full, size, origin, way)
        src = own.at[:, pl.ds(way * half, half)] if step == 0 else dst
        return pltpu.make_async_remote_copy(
            src_ref=src,
            dst_ref=dst,
            send_sem=ring_send.at[i, way, step],
            recv_sem=ring_recv.at[i, way, step],
            device_id=(right if way == 0 else left, code),
            device_id_type=MESH,
        )

    def pass_copy(i, way, step):
        own, full, size = whole[i]
        origin = ring_chip(place - step if way == 0 else place + step) * 2 + core
        dst = part(full, size, origin, way)
        src = own.at[:, pl.ds(way * half, half)] if step == 0 else dst
        return pltpu.make_async_remote_copy(
            src_ref=src,
            dst_ref=dst,
            send_sem=pass_send.at[i, way, step],
            recv_sem=pass_recv.at[i, way, step],
            device_id=(partner, code),
            device_id_type=MESH,
        )

    def own_copy(i):
        own, full, size = whole[i]
        start = pl.multiple_of(dp * size, 16)
        return pltpu.make_async_copy(own, full.at[pl.ds(start, size), :], own_sem.at[i])

    def add_base(origin, way):
        lanes = pl.ds(way * half, half)
        base[:, lanes] += dot_nn(
            temporal[:, pl.ds(pl.multiple_of(origin * depth, 128), depth)],
            proj[pl.ds(pl.multiple_of(origin * depth, 16), depth), lanes],
        )

    for i in range(3):
        for way in range(2):
            ring_copy(i, way, 0).start()
    for i in range(3):
        for way in range(2):
            pass_copy(i, way, 0).start()
        own_copy(i).start()
    base[...] = embedded[...].astype(jnp.float32)
    own_copy(0).wait()
    for way in range(2):
        add_base(dp, way)
    for step in range(1, chips):
        for i in range(3):
            for way in range(2):
                ring_copy(i, way, step - 1).wait_recv()
                if step < chips - 1:
                    ring_copy(i, way, step).start()
                pass_copy(i, way, step).start()
            if i == 0:
                for way in range(2):
                    add_base(ring_chip(place - step if way == 0 else place + step) * 2 + core, way)
                for way in range(2):
                    pass_copy(0, way, step - 1).wait_recv()
                    add_base(
                        ring_chip(place - step + 1 if way == 0 else place + step - 1) * 2 + 1 - core,
                        way,
                    )
    for way in range(2):
        pass_copy(0, way, chips - 1).wait_recv()
        add_base(
            ring_chip(place - chips + 1 if way == 0 else place + chips - 1) * 2 + 1 - core, way
        )

    def swap_copy(i, other):
        target = lax.rem(dp + other, n_dp)
        if i == 0:
            src = temporal.at[:, pl.ds(pl.multiple_of(target * depth, 128), depth)]
            dst = cols_all.at[dp]
        else:
            table, full = ((act_t, act_all), (pre_t, pre_all))[i - 1]
            src = table.at[pl.ds(pl.multiple_of(target * pad, 16), pad), :]
            dst = full.at[dp]
        return pltpu.make_async_remote_copy(
            src_ref=src,
            dst_ref=dst,
            send_sem=swap_send.at[i, other],
            recv_sem=swap_recv.at[i, other],
            device_id=(target, code),
            device_id_type=MESH,
        )

    gathered = (normed_all, slope_all, carry_all)

    def peer_copy(i, other):
        block = gathered[i].at[dp]
        target = lax.rem(dp + 2 * other, n_dp)
        return pltpu.make_async_remote_copy(
            src_ref=block,
            dst_ref=block,
            send_sem=ag_send.at[i, 0, other],
            recv_sem=ag_recv.at[i, 0, other],
            device_id=(target, code),
            device_id_type=MESH,
        )

    def hand_copy(i, other):
        block = gathered[i].at[lax.rem(dp - 2 * other + n_dp, n_dp)]
        return pltpu.make_async_remote_copy(
            src_ref=block,
            dst_ref=block,
            send_sem=ag_send.at[i, 1, other],
            recv_sem=ag_recv.at[i, 1, other],
            device_id=(partner, code),
            device_id_type=MESH,
        )

    def gather_start(i):
        for other in range(1, chips):
            peer_copy(i, other).start()
        hand_copy(i, 0).start()

    def gather_forward(i):
        for other in range(1, chips):
            peer_copy(i, other).wait_recv()
            hand_copy(i, other).start()

    def gather_finish(i):
        for other in range(1, chips):
            peer_copy(i, other).wait_send()
        for other in range(chips):
            hand_copy(i, other).wait()

    def chain_copy(way, c):
        chunk = pl.ds(c * step_rows, step_rows)
        src, dst = ((state, incoming), (carry_out, returning))[way]
        target = lax.rem(code + (1 if way == 0 else n_code - 1), n_code)
        return pltpu.make_async_remote_copy(
            src_ref=src.at[chunk, :],
            dst_ref=dst.at[chunk, :],
            send_sem=chain_send.at[way, c],
            recv_sem=chain_recv.at[way, c],
            device_id=(dp, target),
            device_id_type=MESH,
        )

    first = code == 0
    last = code == n_code - 1

    @pl.when(first)
    def _():
        incoming[...] = jnp.zeros_like(incoming)

    @pl.when(last)
    def _():
        returning[...] = jnp.zeros_like(returning)

    for i in range(1, 3):
        own_copy(i).wait()
        for way in range(2):
            for step in range(chips):
                pass_copy(i, way, step).wait_recv()
    for other in range(1, n_dp):
        swap_copy(0, other).start()
    cols_all[dp] = temporal[:, pl.ds(pl.multiple_of(dp * depth, 128), depth)]

    tiles = hidden // TILE
    rest = hidden - tiles * TILE

    def over_tiles(body):
        def turn(t, carry):
            body(pl.multiple_of(t * TILE, TILE), TILE)
            return carry

        lax.fori_loop(0, tiles, turn, 0)
        if rest:
            body(tiles * TILE, rest)

    for c in range(CHUNKS):
        chunk = pl.ds(c * step_rows, step_rows)

        @pl.when(jnp.logical_not(first))
        def _():
            chain_copy(0, c).wait_recv()

        resid = base[chunk, :] + incoming[chunk, :].astype(jnp.float32)
        base[chunk, :] = resid
        scale = lax.rsqrt(jnp.mean(resid * resid, axis=-1, keepdims=True) + EPS)
        scale_ref[chunk, :] = jnp.broadcast_to(scale, (step_rows, 128))
        normed_all[dp, chunk, :] = (resid * scale).astype(jnp.bfloat16)
        acc[chunk, :] = resid

        def forward(start, size):
            lanes = pl.ds(start, size)
            pre = dot_nt(normed_all[dp, chunk, :], w1[lanes, :])
            deriv[chunk, lanes] = pre
            active = (pre * jax.nn.sigmoid(pre)).astype(jnp.bfloat16)
            acc[chunk, :] += dot_nn(active, w2[lanes, :])

        over_tiles(forward)
        state[chunk, :] = acc[chunk, :].astype(jnp.bfloat16)

        @pl.when(jnp.logical_not(last))
        def _():
            chain_copy(0, c).start()

    gather_start(0)

    def slopes(start, size):
        lanes = pl.ds(start, size)
        pre = deriv[:, lanes]
        sigma = jax.nn.sigmoid(pre)
        active = pre * sigma
        deriv[:, lanes] = sigma * (1.0 + pre * (1.0 - sigma))
        act_t[lanes, :] = active.T.astype(jnp.bfloat16)

    over_tiles(slopes)
    for other in range(1, n_dp):
        swap_copy(1, other).start()
    act_all[dp] = act_t[pl.ds(pl.multiple_of(dp * pad, 16), pad), :]
    gather_forward(0)

    for c in range(CHUNKS):
        chunk = pl.ds(c * step_rows, step_rows)

        @pl.when(jnp.logical_not(last))
        def _():
            chain_copy(1, c).wait_recv()

        slope = cot_ref[chunk, :].astype(jnp.float32) + returning[chunk, :].astype(jnp.float32)
        slope_all[dp, chunk, :] = slope.astype(jnp.bfloat16)
        acc[chunk, :] = jnp.zeros((step_rows, width), jnp.float32)

        def backward(start, size):
            lanes = pl.ds(start, size)
            back = dot_nt(slope_all[dp, chunk, :], w2[lanes, :])
            pre_slope = back * deriv[chunk, lanes]
            deriv[chunk, lanes] = pre_slope
            acc[chunk, :] += dot_nn(pre_slope.astype(jnp.bfloat16), w1[lanes, :])

        over_tiles(backward)
        norm_slope = acc[chunk, :]
        scale = scale_ref[chunk, 0:1]
        unit = base[chunk, :] * scale
        slope = cot_ref[chunk, :].astype(jnp.float32) + returning[chunk, :].astype(jnp.float32)
        carried = (
            slope
            + scale * (norm_slope - unit * jnp.mean(norm_slope * unit, axis=-1, keepdims=True))
        ).astype(jnp.bfloat16)
        carry_out[chunk, :] = carried
        carry_all[dp, chunk, :] = carried

        @pl.when(jnp.logical_not(first))
        def _():
            chain_copy(1, c).start()

    gather_start(2)
    gather_start(1)

    quarter = term.shape[2]
    per = quarter // depth

    def terms(j, carry):
        rows_j = pl.ds(pl.multiple_of(j * depth, 16), depth)
        value = dot_nt(carry_all[dp], proj[rows_j, :]).astype(jnp.bfloat16)
        term[j // per, :, pl.ds(pl.multiple_of(lax.rem(j, per) * depth, 128), depth)] = value
        return carry

    lax.fori_loop(0, n_dp, terms, 0)

    def term_copy(other):
        target = lax.rem(code + other, n_code)
        return pltpu.make_async_remote_copy(
            src_ref=term.at[target],
            dst_ref=term_in.at[other],
            send_sem=term_send.at[other],
            recv_sem=term_recv.at[other],
            device_id=(dp, target),
            device_id_type=MESH,
        )

    for other in range(1, n_code):
        term_copy(other).start()

    def turn_over(start, size):
        lanes = pl.ds(start, size)
        pre_t[lanes, :] = deriv[:, lanes].T.astype(jnp.bfloat16)

    over_tiles(turn_over)
    for other in range(1, n_dp):
        swap_copy(2, other).start()
    pre_all[dp] = pre_t[pl.ds(pl.multiple_of(dp * pad, 16), pad), :]

    gather_forward(2)
    gather_forward(1)
    total = term[code].astype(jnp.float32)
    for other in range(1, n_code):
        term_copy(other).wait_recv()
        total += term_in[other].astype(jnp.float32)
    temporal_grad[...] = total.astype(jnp.bfloat16)

    for i in range(3):
        for way in range(2):
            for step in range(chips - 1):
                ring_copy(i, way, step).wait_send()
            for step in range(chips):
                pass_copy(i, way, step).wait_send()
    for c in range(CHUNKS):

        @pl.when(jnp.logical_not(last))
        def _():
            chain_copy(0, c).wait_send()

        @pl.when(jnp.logical_not(first))
        def _():
            chain_copy(1, c).wait_send()

    for i in range(3):
        gather_finish(i)
        for other in range(1, n_dp):
            swap_copy(i, other).wait()
    for other in range(1, n_code):
        term_copy(other).wait_send()


def per_device(
    temporal_out, depth_in, embed, depth_w1, depth_w2, audio_tokens, barge_mask, out_grad
):
    dp_index = lax.axis_index("dp")
    n_code = lax.axis_size("code")
    n_dp = lax.axis_size("dp")
    rows, wide = temporal_out.shape
    depth, width = depth_in.shape[1:]
    share = depth_w1.shape[2]
    pad = -(-share // 16) * 16
    hidden = pad * n_dp
    quarter = wide // n_code
    chips = n_dp // 2
    table = embed[0]
    token_all = audio_tokens[:, 0]
    token_own = lax.dynamic_slice_in_dim(token_all, dp_index * rows, rows, 0)
    embedded = jnp.take(table, token_own, axis=0)
    cotangent = out_grad[:, 0, :] * barge_mask.astype(jnp.bfloat16)[:, None]
    w1_own = jnp.pad(depth_w1[0].T, ((0, pad - share), (0, 0)))
    w2_own = jnp.pad(depth_w2[0].T, ((0, pad - share), (0, 0)))

    bf16, f32 = jnp.bfloat16, jnp.float32
    vmem = pl.BlockSpec(memory_space=pltpu.VMEM)
    hbm = pl.BlockSpec(memory_space=pl.ANY)
    dma = pltpu.SemaphoreType.DMA
    out_shape = (
        jax.ShapeDtypeStruct((rows, quarter), bf16),
        jax.ShapeDtypeStruct((n_dp, rows, depth), bf16),
        jax.ShapeDtypeStruct((n_dp, rows, width), bf16),
        jax.ShapeDtypeStruct((n_dp, rows, width), bf16),
        jax.ShapeDtypeStruct((n_dp, rows, width), bf16),
        jax.ShapeDtypeStruct((n_dp, pad, rows), bf16),
        jax.ShapeDtypeStruct((n_dp, pad, rows), bf16),
    )
    temporal_grad, cols_all, normed_all, slope_all, carry_all, act_all, pre_all = pl.pallas_call(
        functools.partial(chain_kernel, n_dp, n_code),
        out_shape=out_shape,
        in_specs=[vmem, vmem, vmem, hbm, hbm, hbm],
        out_specs=(vmem,) * 7,
        scratch_shapes=[
            pltpu.VMEM((wide, width), bf16),
            pltpu.VMEM((hidden, width), bf16),
            pltpu.VMEM((hidden, width), bf16),
            pltpu.VMEM((rows, width), f32),
            pltpu.VMEM((rows, width), f32),
            pltpu.VMEM((rows, width), bf16),
            pltpu.VMEM((rows, width), bf16),
            pltpu.VMEM((rows, width), bf16),
            pltpu.VMEM((rows, width), bf16),
            pltpu.VMEM((rows, hidden), f32),
            pltpu.VMEM((hidden, rows), bf16),
            pltpu.VMEM((hidden, rows), bf16),
            pltpu.VMEM((rows, 128), f32),
            pltpu.VMEM((n_code, rows, quarter), bf16),
            pltpu.VMEM((n_code, rows, quarter), bf16),
            dma((3, 2, chips)),
            dma((3, 2, chips)),
            dma((3, 2, chips)),
            dma((3, 2, chips)),
            dma((3,)),
            dma((2, CHUNKS)),
            dma((2, CHUNKS)),
            dma((3, 2, chips)),
            dma((3, 2, chips)),
            dma((3, n_dp)),
            dma((3, n_dp)),
            dma((n_code,)),
            dma((n_code,)),
        ],
        compiler_params=pltpu.CompilerParams(
            collective_id=0, has_side_effects=True, vmem_limit_bytes=60 * 1024 * 1024
        ),
        name="depth_chain",
    )(temporal_out, embedded, cotangent, depth_in[0], w1_own, w2_own)

    def over_rows(left, right):
        return lax.dot_general(
            left, right, (((0,), (0,)), ((), ())), preferred_element_type=jnp.float32
        )

    frames = n_dp * rows
    normed = normed_all.reshape(frames, width)
    slope = slope_all.reshape(frames, width)
    carry = carry_all.reshape(frames, width)
    columns = cols_all.reshape(frames, depth)
    pre_rows = pre_all[:, :share, :].transpose(0, 2, 1).reshape(frames, share)
    act_rows = act_all[:, :share, :].transpose(0, 2, 1).reshape(frames, share)
    first_grad = over_rows(normed, pre_rows).astype(bf16)
    second_grad = over_rows(slope, act_rows).astype(bf16)
    proj_grad = over_rows(columns, carry).astype(bf16)
    vocab_local = table.shape[0] // n_dp
    vocab_ids = lax.broadcasted_iota(jnp.int32, (1, vocab_local), 1) + dp_index * vocab_local
    onehot = (token_all[:, None] == vocab_ids).astype(bf16)
    table_grad = over_rows(onehot, carry).astype(bf16)
    return (
        temporal_grad,
        proj_grad[None],
        table_grad[None],
        first_grad[None],
        second_grad[None],
    )


def solution(mesh):
    in_specs = (
        P("dp", None),
        P("code", "dp", None),
        P("code", None, None),
        P("code", None, "dp"),
        P("code", None, "dp"),
        P(None, "code"),
        P("dp"),
        P("dp", "code", None),
    )
    out_specs = (
        P("dp", "code"),
        P("code", "dp", None),
        P("code", "dp", None),
        P("code", None, "dp"),
        P("code", None, "dp"),
    )
    return jax.shard_map(
        per_device, mesh=mesh, in_specs=in_specs, out_specs=out_specs, check_vma=False
    )
```

time: 455 us -> 218 us (0.48)
  waiting for transfers between devices: 294 us -> 0 us
  Pallas kernels: 0 us -> 199 us
  matrix products: 95.1 us -> 9.61 us
  starting transfers between devices: 19.6 us -> 0 us
  local copies, waits for them, and re-layouts: 22.4 us -> 5.37 us
  between operations: 14.3 us -> 0.71 us
  other arithmetic: 8.67 us -> 3.16 us
    pallas_call x0 -> x1, Pallas kernels: none -> 199 us  [per_device(): pl.pallas_call(functools.partial(chain_kernel, n_dp, n_code), out_shape=o...]
    all_gather x4 -> x0, waiting for transfers between devices: 122 us -> none  [the longest x1 49.8 us: per_device(): projection = lax.all_gather(depth_in[0], 'dp', axis=0, tiled=True)]
    reduce_scatter x3 -> x0, waiting for transfers between devices: 117 us -> none  [the longest x1 56 us: per_device(): lax.psum_scatter(contract_rows(normed, pre_slope).astype(jnp.bfloat16), '...]
    dot_general x15 -> x4, matrix products: 95.1 us -> 9.61 us  [over_rows(): lax.dot_general(left, right, (((0,), (0,)), ((), ())), preferred_element_...]
    ppermute x6 -> x0, waiting for transfers between devices: 38.1 us -> none  [shifted(): return lax.ppermute(block, axis, route)]
    ppermute x6 -> x0, starting transfers between devices: 15.8 us -> none  [shifted(): return lax.ppermute(block, axis, route)]
    all_to_all x1 -> x0, waiting for transfers between devices: 15.3 us -> none  [per_device(): lax.all_to_all(temporal_out, 'dp', split_axis=1, concat_axis=0, tiled=True)]
    while x2 -> x0, local copies, waits for them, and re-layouts: 12.8 us -> none  [per_device(): incoming = lax.fori_loop(0, n_code - 1, forward_turn, start_state)]
  transfers between devices with their start and end apart: 14 -> 0, of which waited for: 13 -> 0; matrix products, arithmetic and copies ran while one was open for 10% -> 0% of each run, Pallas kernels for 0% -> 0%
where the time goes in v1:
time: 218 us
  Pallas kernels  199 us (91%)
  matrix products  9.61 us (4%)
  local copies, waits for them, and re-layouts  5.37 us (2%)
  other arithmetic  3.16 us (1%)
    pallas_call x1, Pallas kernels, per_device(): pl.pallas_call(functools.partial(chain_kernel, n_dp, n_code), out_shape=o...  199 us
    dot_general x4, matrix products, over_rows(): lax.dot_general(left, right, (((0,), (0,)), ((), ())), preferred_element_...  9.61 us

profile of v1, /device:TPU:0, one launch (start us, length us, event | category | flops | bytes accessed | tf_op | source)
XLA Modules:
  0.0 217.7 jit_solution(3776968314456156555)
XLA Ops:
  0.6 0.0 copy-start
  0.6 0.0 copy-start.3
  0.7 1.6 copy-done
  2.2 0.7 convert_element_type.19
  2.9 0.7 and_bitcast_fusion
  3.6 0.0 copy-start.4
  3.6 0.9 gather_fusion
  4.4 1.8 bitcast_multiply_fusion
  6.3 0.0 copy-done.3
  6.3 0.8 pad.7.w1_own
  7.1 0.0 copy-done.4
  7.1 0.9 pad.8.w2_own
  8.0 0.0 copy-start.6
  8.0 198.9 %depth_chain.1 = (bf16[128,1024]{1,0:T(8,128)(2,1)}, bf16[8,128,512]{2,1,0:T(8,128)(2,1)}, bf16[8,128,1024]{2,1,0:T(8,128)(2,1)}, bf16[8,128,1024]{2,1,0:T(8,128...) custom-call(bf16[128,4096]{1,0:T(8,128)(2,1)} %temporal.1, ...), custom_call_target="tpu_custom_call" | custom-call | tf_op jit(solution)/shard_map/depth_chain/pallas_call | solution.py:474
  206.8 0.0 copy-start.8
  206.8 0.0 copy-done.6
  206.9 3.1 %fusion.5 = bf16[1,128,1024]{2,1,0:T(8,128)(2,1)} fusion(bf16[1024,1024]{1,0:T(8,128)(2,1)} %bitcast.51, s32[128]{0:T(128)S(1)} %iota_add_fusion, s32[1024]{0:T(1024)S(1)} %bitcast.55), kind=kOutput, calls=%fused_computation.10 | convolution fusion | flops 268697600 | bytes 2363904 | tf_op jit(solution)/shard_map/dot_general | solution.py:516
  210.0 0.0 copy-done.8
  210.0 0.0 copy-start.7
  210.0 0.0 copy-start.9
  210.0 2.7 %fusion.4 = bf16[1,1024,264]{1,2,0:T(8,128)(2,1)} fusion(bf16[8,128,1024]{2,1,0:T(8,128)(2,1)S(1)} %copy-done.8, bf16[8,272,128]{2,1,0:T(8,128)(2,1)} %get-tuple-element.16), kind=kOutput, calls=%fused_computation.8 | convolution fusion | flops 553918464 | bytes 3178496 | tf_op jit(solution)/shard_map/dot_general | solution.py:516
  212.7 0.0 copy-done.7
  212.7 0.0 copy-done.9
  212.7 0.0 copy-start.1
  212.7 0.0 copy-start.2
  212.7 1.5 fusion.3
  214.2 0.1 copy-done.1
  214.3 0.5 copy-done.2
  214.8 0.0 copy-start.5
  214.8 2.2 %fusion = bf16[1,512,1024]{2,1,0:T(8,128)(2,1)} fusion(bf16[8,128,512]{2,1,0:T(8,128)(2,1)S(1)} %copy-done.2, bf16[8,128,1024]{2,1,0:T(8,128)(2,1)S(1)} %copy-done.1), kind=kOutput, calls=%fused_computation.4 | convolution fusion | flops 1074266112 | bytes 4194304 | tf_op jit(solution)/shard_map/dot_general | solution.py:516
  217.0 0.0 copy-done.5
  217.0 0.7 copy.16
  (2 shorter events, 0.0 us)
Async XLA Ops:
  0.6 1.6 copy-start
  0.6 5.6 %copy-start.3 = (bf16[1,1024,264]{1,2,0:T(8,128)(2,1)S(1)}, bf16[1,1024,264]{1,2,0:T(8,128)(2,1)}, u32[]{:S(2)}) copy-start(bf16[1,1024,264]{1,2,0:T(8,128)(2,1)} %param.11) | copy-start | bytes 1622020
  3.6 3.6 %copy-start.4 = (bf16[1,1024,264]{1,2,0:T(8,128)(2,1)S(1)}, bf16[1,1024,264]{1,2,0:T(8,128)(2,1)}, u32[]{:S(2)}) copy-start(bf16[1,1024,264]{1,2,0:T(8,128)(2,1)} %param.12) | copy-start | bytes 1622020
  8.0 198.9 %copy-start.6 = (s32[1024,1]{0,1:T(1,128)S(1)}, s32[1024,1]{0,1:T(1,128)}, u32[]{:S(2)}) copy-start(s32[1024,1]{0,1:T(1,128)} %param.13) | copy-start | bytes 12292
  206.8 3.1 %copy-start.8 = (bf16[8,128,1024]{2,1,0:T(8,128)(2,1)S(1)}, bf16[8,128,1024]{2,1,0:T(8,128)(2,1)}, u32[]{:S(2)}) copy-start(bf16[8,128,1024]{2,1,0:T(8,128)(2,1)} %get-tuple-element.15) | copy-start | bytes 6291460
  210.0 2.7 %copy-start.7 = (bf16[8,128,1024]{2,1,0:T(8,128)(2,1)S(1)}, bf16[8,128,1024]{2,1,0:T(8,128)(2,1)}, u32[]{:S(2)}) copy-start(bf16[8,128,1024]{2,1,0:T(8,128)(2,1)} %get-tuple-element.17) | copy-start | bytes 6291460
  210.0 2.7 %copy-start.9 = (bf16[8,272,128]{2,1,0:T(8,128)(2,1)S(1)}, bf16[8,272,128]{2,1,0:T(8,128)(2,1)}, u32[]{:S(2)}) copy-start(bf16[8,272,128]{2,1,0:T(8,128)(2,1)} %get-tuple-element.18) | copy-start | bytes 1671172
  212.7 1.6 copy-start.1
  212.7 2.1 copy-start.2
  214.8 2.2 %copy-start.5 = (bf16[128,1024]{1,0:T(8,128)(2,1)S(1)}, bf16[128,1024]{1,0:T(8,128)(2,1)}, u32[]{:S(2)}) copy-start(bf16[128,1024]{1,0:T(8,128)(2,1)} %get-tuple-element.28) | copy-start | bytes 786436

commit v2 on v1

--- a/solution.py
+++ b/solution.py
@@ -343,6 +343,8 @@
 
         slope = cot_ref[chunk, :].astype(jnp.float32) + returning[chunk, :].astype(jnp.float32)
         slope_all[dp, chunk, :] = slope.astype(jnp.bfloat16)
+        if c == CHUNKS - 1:
+            gather_start(1)
         acc[chunk, :] = jnp.zeros((step_rows, width), jnp.float32)
 
         def backward(start, size):
@@ -369,18 +371,10 @@
             chain_copy(1, c).start()
 
     gather_start(2)
-    gather_start(1)
 
     quarter = term.shape[2]
     per = quarter // depth
-
-    def terms(j, carry):
-        rows_j = pl.ds(pl.multiple_of(j * depth, 16), depth)
-        value = dot_nt(carry_all[dp], proj[rows_j, :]).astype(jnp.bfloat16)
-        term[j // per, :, pl.ds(pl.multiple_of(lax.rem(j, per) * depth, 128), depth)] = value
-        return carry
-
-    lax.fori_loop(0, n_dp, terms, 0)
+    early = code * 2 < n_code
 
     def term_copy(other):
         target = lax.rem(code + other, n_code)
@@ -393,8 +387,18 @@
             device_id_type=MESH,
         )
 
-    for other in range(1, n_code):
-        term_copy(other).start()
+    for other in reversed(range(n_code)):
+        target = lax.rem(code + other, n_code)
+        for piece in range(per):
+            start = pl.multiple_of(target * quarter + piece * depth, 16)
+            term[target, :, piece * depth : (piece + 1) * depth] = dot_nt(
+                carry_all[dp], proj[pl.ds(start, depth), :]
+            ).astype(jnp.bfloat16)
+        if other:
+
+            @pl.when(early)
+            def _():
+                term_copy(other).start()
 
     def turn_over(start, size):
         lanes = pl.ds(start, size)
@@ -405,8 +409,14 @@
         swap_copy(2, other).start()
     pre_all[dp] = pre_t[pl.ds(pl.multiple_of(dp * pad, 16), pad), :]
 
+    gather_forward(1)
     gather_forward(2)
-    gather_forward(1)
+
+    @pl.when(jnp.logical_not(early))
+    def _():
+        for other in range(1, n_code):
+            term_copy(other).start()
+
     total = term[code].astype(jnp.float32)
     for other in range(1, n_code):
         term_copy(other).wait_recv()

time: 218 us -> 202 us (0.927)
  Pallas kernels: 199 us -> 183 us
    pallas_call x1, Pallas kernels: 199 us -> 183 us  [per_device(): pl.pallas_call(functools.partial(chain_kernel, n_dp, n_code), out_shape=o...]
where the time goes in v2:
time: 202 us
  Pallas kernels  183 us (91%)
  matrix products  9.63 us (5%)
  local copies, waits for them, and re-layouts  5.36 us (3%)
  other arithmetic  3.16 us (2%)
    pallas_call x1, Pallas kernels, per_device(): pl.pallas_call(functools.partial(chain_kernel, n_dp, n_code), out_shape=o...  183 us
    dot_general x4, matrix products, over_rows(): lax.dot_general(left, right, (((0,), (0,)), ((), ())), preferred_element_...  9.63 us

profile of v2, /device:TPU:0, one launch (start us, length us, event | category | flops | bytes accessed | tf_op | source)
XLA Modules:
  0.0 202.2 jit_solution(11392963948073556634)
XLA Ops:
  0.6 0.0 copy-start
  0.6 0.0 copy-start.3
  0.7 1.6 copy-done
  2.2 0.7 convert_element_type.19
  2.9 0.7 and_bitcast_fusion
  3.6 0.0 copy-start.4
  3.6 0.9 gather_fusion
  4.4 1.8 bitcast_multiply_fusion
  6.3 0.0 copy-done.3
  6.3 0.8 pad.7.w1_own
  7.1 0.0 copy-done.4
  7.1 0.9 pad.8.w2_own
  8.0 0.0 copy-start.6
  8.0 183.3 %depth_chain.1 = (bf16[128,1024]{1,0:T(8,128)(2,1)}, bf16[8,128,512]{2,1,0:T(8,128)(2,1)}, bf16[8,128,1024]{2,1,0:T(8,128)(2,1)}, bf16[8,128,1024]{2,1,0:T(8,128...) custom-call(bf16[128,4096]{1,0:T(8,128)(2,1)} %temporal.1, ...), custom_call_target="tpu_custom_call" | custom-call | tf_op jit(solution)/shard_map/depth_chain/pallas_call | solution.py:484
  191.3 0.0 copy-start.8
  191.3 0.0 copy-done.6
  191.3 3.1 %fusion.5 = bf16[1,128,1024]{2,1,0:T(8,128)(2,1)} fusion(bf16[1024,1024]{1,0:T(8,128)(2,1)} %bitcast.51, s32[128]{0:T(128)S(1)} %iota_add_fusion, s32[1024]{0:T(1024)S(1)} %bitcast.55), kind=kOutput, calls=%fused_computation.10 | convolution fusion | flops 268697600 | bytes 2363904 | tf_op jit(solution)/shard_map/dot_general | solution.py:526
  194.4 0.0 copy-done.8
  194.4 0.0 copy-start.7
  194.4 0.0 copy-start.9
  194.5 2.7 %fusion.4 = bf16[1,1024,264]{1,2,0:T(8,128)(2,1)} fusion(bf16[8,128,1024]{2,1,0:T(8,128)(2,1)S(1)} %copy-done.8, bf16[8,272,128]{2,1,0:T(8,128)(2,1)} %get-tuple-element.16), kind=kOutput, calls=%fused_computation.8 | convolution fusion | flops 553918464 | bytes 3178496 | tf_op jit(solution)/shard_map/dot_general | solution.py:526
  197.2 0.0 copy-done.7
  197.2 0.0 copy-done.9
  197.2 0.0 copy-start.1
  197.2 0.0 copy-start.2
  197.2 1.5 fusion.3
  198.7 0.0 copy-done.1
  198.8 0.5 copy-done.2
  199.2 0.0 copy-start.5
  199.2 2.2 %fusion = bf16[1,512,1024]{2,1,0:T(8,128)(2,1)} fusion(bf16[8,128,512]{2,1,0:T(8,128)(2,1)S(1)} %copy-done.2, bf16[8,128,1024]{2,1,0:T(8,128)(2,1)S(1)} %copy-done.1), kind=kOutput, calls=%fused_computation.4 | convolution fusion | flops 1074266112 | bytes 4194304 | tf_op jit(solution)/shard_map/dot_general | solution.py:526
  201.5 0.0 copy-done.5
  201.5 0.7 copy.16
  (2 shorter events, 0.0 us)
Async XLA Ops:
  0.6 1.6 copy-start
  0.6 5.6 %copy-start.3 = (bf16[1,1024,264]{1,2,0:T(8,128)(2,1)S(1)}, bf16[1,1024,264]{1,2,0:T(8,128)(2,1)}, u32[]{:S(2)}) copy-start(bf16[1,1024,264]{1,2,0:T(8,128)(2,1)} %param.11) | copy-start | bytes 1622020
  3.6 3.6 %copy-start.4 = (bf16[1,1024,264]{1,2,0:T(8,128)(2,1)S(1)}, bf16[1,1024,264]{1,2,0:T(8,128)(2,1)}, u32[]{:S(2)}) copy-start(bf16[1,1024,264]{1,2,0:T(8,128)(2,1)} %param.12) | copy-start | bytes 1622020
  8.0 183.4 %copy-start.6 = (s32[1024,1]{0,1:T(1,128)S(1)}, s32[1024,1]{0,1:T(1,128)}, u32[]{:S(2)}) copy-start(s32[1024,1]{0,1:T(1,128)} %param.13) | copy-start | bytes 12292
  191.3 3.1 %copy-start.8 = (bf16[8,128,1024]{2,1,0:T(8,128)(2,1)S(1)}, bf16[8,128,1024]{2,1,0:T(8,128)(2,1)}, u32[]{:S(2)}) copy-start(bf16[8,128,1024]{2,1,0:T(8,128)(2,1)} %get-tuple-element.15) | copy-start | bytes 6291460
  194.4 2.7 %copy-start.7 = (bf16[8,128,1024]{2,1,0:T(8,128)(2,1)S(1)}, bf16[8,128,1024]{2,1,0:T(8,128)(2,1)}, u32[]{:S(2)}) copy-start(bf16[8,128,1024]{2,1,0:T(8,128)(2,1)} %get-tuple-element.17) | copy-start | bytes 6291460
  194.4 2.7 %copy-start.9 = (bf16[8,272,128]{2,1,0:T(8,128)(2,1)S(1)}, bf16[8,272,128]{2,1,0:T(8,128)(2,1)}, u32[]{:S(2)}) copy-start(bf16[8,272,128]{2,1,0:T(8,128)(2,1)} %get-tuple-element.18) | copy-start | bytes 1671172
  197.2 1.6 copy-start.1
  197.2 2.1 %copy-start.2 = (bf16[8,128,512]{2,1,0:T(8,128)(2,1)S(1)}, bf16[8,128,512]{2,1,0:T(8,128)(2,1)}, u32[]{:S(2)}) copy-start(bf16[8,128,512]{2,1,0:T(8,128)(2,1)} %get-tuple-element.13) | copy-start | bytes 3145732
  199.2 2.2 %copy-start.5 = (bf16[128,1024]{1,0:T(8,128)(2,1)S(1)}, bf16[128,1024]{1,0:T(8,128)(2,1)}, u32[]{:S(2)}) copy-start(bf16[128,1024]{1,0:T(8,128)(2,1)} %get-tuple-element.28) | copy-start | bytes 786436

commit v3 on v2

--- a/solution.py
+++ b/solution.py
@@ -332,7 +332,11 @@
     for other in range(1, n_dp):
         swap_copy(1, other).start()
     act_all[dp] = act_t[pl.ds(pl.multiple_of(dp * pad, 16), pad), :]
-    gather_forward(0)
+
+    @pl.when(first)
+    def _():
+        gather_forward(0)
+
 
     for c in range(CHUNKS):
         chunk = pl.ds(c * step_rows, step_rows)
@@ -371,6 +375,10 @@
             chain_copy(1, c).start()
 
     gather_start(2)
+
+    @pl.when(jnp.logical_not(first))
+    def _():
+        gather_forward(0)
 
     quarter = term.shape[2]
     per = quarter // depth

time: 202 us -> 192 us (0.950)
  Pallas kernels: 183 us -> 172 us
    pallas_call x1, Pallas kernels: 183 us -> 172 us  [per_device(): pl.pallas_call(functools.partial(chain_kernel, n_dp, n_code), out_shape=o...]
where the time goes in v3:
time: 192 us; the launch traced here: 191 us
  Pallas kernels  172 us (90%)
  matrix products  9.63 us (5%)
  local copies, waits for them, and re-layouts  5.36 us (3%)
  other arithmetic  3.16 us (2%)
    pallas_call x1, Pallas kernels, per_device(): pl.pallas_call(functools.partial(chain_kernel, n_dp, n_code), out_shape=o...  172 us
    dot_general x4, matrix products, over_rows(): lax.dot_general(left, right, (((0,), (0,)), ((), ())), preferred_element_...  9.63 us

profile of v3, /device:TPU:0, one launch (start us, length us, event | category | flops | bytes accessed | tf_op | source)
XLA Modules:
  0.0 190.9 jit_solution(5976119653033050206)
XLA Ops:
  0.6 0.0 copy-start
  0.6 0.0 copy-start.3
  0.7 1.6 copy-done
  2.2 0.7 convert_element_type.19
  2.9 0.7 and_bitcast_fusion
  3.6 0.0 copy-start.4
  3.6 0.9 gather_fusion
  4.4 1.8 bitcast_multiply_fusion
  6.3 0.0 copy-done.3
  6.3 0.8 pad.7.w1_own
  7.1 0.0 copy-done.4
  7.1 0.9 pad.8.w2_own
  8.0 0.0 copy-start.6
  8.0 172.0 %depth_chain.1 = (bf16[128,1024]{1,0:T(8,128)(2,1)}, bf16[8,128,512]{2,1,0:T(8,128)(2,1)}, bf16[8,128,1024]{2,1,0:T(8,128)(2,1)}, bf16[8,128,1024]{2,1,0:T(8,128...) custom-call(bf16[128,4096]{1,0:T(8,128)(2,1)} %temporal.1, ...), custom_call_target="tpu_custom_call" | custom-call | tf_op jit(solution)/shard_map/depth_chain/pallas_call | solution.py:492
  180.0 0.0 copy-start.8
  180.0 0.0 copy-done.6
  180.0 3.1 %fusion.5 = bf16[1,128,1024]{2,1,0:T(8,128)(2,1)} fusion(bf16[1024,1024]{1,0:T(8,128)(2,1)} %bitcast.51, s32[128]{0:T(128)S(1)} %iota_add_fusion, s32[1024]{0:T(1024)S(1)} %bitcast.55), kind=kOutput, calls=%fused_computation.10 | convolution fusion | flops 268697600 | bytes 2363904 | tf_op jit(solution)/shard_map/dot_general | solution.py:534
  183.1 0.0 copy-done.8
  183.1 0.0 copy-start.7
  183.1 0.0 copy-start.9
  183.1 2.7 %fusion.4 = bf16[1,1024,264]{1,2,0:T(8,128)(2,1)} fusion(bf16[8,128,1024]{2,1,0:T(8,128)(2,1)S(1)} %copy-done.8, bf16[8,272,128]{2,1,0:T(8,128)(2,1)} %get-tuple-element.16), kind=kOutput, calls=%fused_computation.8 | convolution fusion | flops 553918464 | bytes 3178496 | tf_op jit(solution)/shard_map/dot_general | solution.py:534
  185.8 0.0 copy-done.7
  185.8 0.0 copy-done.9
  185.9 0.0 copy-start.1
  185.9 0.0 copy-start.2
  185.9 1.5 fusion.3
  187.4 0.0 copy-done.1
  187.4 0.5 copy-done.2
  187.9 0.0 copy-start.5
  187.9 2.2 %fusion = bf16[1,512,1024]{2,1,0:T(8,128)(2,1)} fusion(bf16[8,128,512]{2,1,0:T(8,128)(2,1)S(1)} %copy-done.2, bf16[8,128,1024]{2,1,0:T(8,128)(2,1)S(1)} %copy-done.1), kind=kOutput, calls=%fused_computation.4 | convolution fusion | flops 1074266112 | bytes 4194304 | tf_op jit(solution)/shard_map/dot_general | solution.py:534
  190.1 0.0 copy-done.5
  190.2 0.7 copy.16
  (2 shorter events, 0.0 us)
Async XLA Ops:
  0.6 1.6 copy-start
  0.6 5.6 %copy-start.3 = (bf16[1,1024,264]{1,2,0:T(8,128)(2,1)S(1)}, bf16[1,1024,264]{1,2,0:T(8,128)(2,1)}, u32[]{:S(2)}) copy-start(bf16[1,1024,264]{1,2,0:T(8,128)(2,1)} %param.11) | copy-start | bytes 1622020
  3.6 3.6 %copy-start.4 = (bf16[1,1024,264]{1,2,0:T(8,128)(2,1)S(1)}, bf16[1,1024,264]{1,2,0:T(8,128)(2,1)}, u32[]{:S(2)}) copy-start(bf16[1,1024,264]{1,2,0:T(8,128)(2,1)} %param.12) | copy-start | bytes 1622020
  8.0 172.0 %copy-start.6 = (s32[1024,1]{0,1:T(1,128)S(1)}, s32[1024,1]{0,1:T(1,128)}, u32[]{:S(2)}) copy-start(s32[1024,1]{0,1:T(1,128)} %param.13) | copy-start | bytes 12292
  180.0 3.1 %copy-start.8 = (bf16[8,128,1024]{2,1,0:T(8,128)(2,1)S(1)}, bf16[8,128,1024]{2,1,0:T(8,128)(2,1)}, u32[]{:S(2)}) copy-start(bf16[8,128,1024]{2,1,0:T(8,128)(2,1)} %get-tuple-element.15) | copy-start | bytes 6291460
  183.1 2.7 %copy-start.7 = (bf16[8,128,1024]{2,1,0:T(8,128)(2,1)S(1)}, bf16[8,128,1024]{2,1,0:T(8,128)(2,1)}, u32[]{:S(2)}) copy-start(bf16[8,128,1024]{2,1,0:T(8,128)(2,1)} %get-tuple-element.17) | copy-start | bytes 6291460
  183.1 2.7 %copy-start.9 = (bf16[8,272,128]{2,1,0:T(8,128)(2,1)S(1)}, bf16[8,272,128]{2,1,0:T(8,128)(2,1)}, u32[]{:S(2)}) copy-start(bf16[8,272,128]{2,1,0:T(8,128)(2,1)} %get-tuple-element.18) | copy-start | bytes 1671172
  185.9 1.6 copy-start.1
  185.9 2.1 %copy-start.2 = (bf16[8,128,512]{2,1,0:T(8,128)(2,1)S(1)}, bf16[8,128,512]{2,1,0:T(8,128)(2,1)}, u32[]{:S(2)}) copy-start(bf16[8,128,512]{2,1,0:T(8,128)(2,1)} %get-tuple-element.13) | copy-start | bytes 3145732
  187.9 2.2 %copy-start.5 = (bf16[128,1024]{1,0:T(8,128)(2,1)S(1)}, bf16[128,1024]{1,0:T(8,128)(2,1)}, u32[]{:S(2)}) copy-start(bf16[128,1024]{1,0:T(8,128)(2,1)} %get-tuple-element.28) | copy-start | bytes 786436

commit v4 on v3

--- a/solution.py
+++ b/solution.py
@@ -204,10 +204,16 @@
             device_id_type=MESH,
         )
 
-    gathered = (normed_all, slope_all, carry_all)
+    gathered = [(normed_all, 0, rows), (slope_all, 0, rows)] + [
+        (carry_all, c * step_rows, step_rows) for c in range(CHUNKS)
+    ]
+
+    def gather_block(i, owner):
+        full, start, size = gathered[i]
+        return full.at[owner, pl.ds(start, size), :]
 
     def peer_copy(i, other):
-        block = gathered[i].at[dp]
+        block = gather_block(i, dp)
         target = lax.rem(dp + 2 * other, n_dp)
         return pltpu.make_async_remote_copy(
             src_ref=block,
@@ -219,7 +225,7 @@
         )
 
     def hand_copy(i, other):
-        block = gathered[i].at[lax.rem(dp - 2 * other + n_dp, n_dp)]
+        block = gather_block(i, lax.rem(dp - 2 * other + n_dp, n_dp))
         return pltpu.make_async_remote_copy(
             src_ref=block,
             dst_ref=block,
@@ -374,7 +380,7 @@
         def _():
             chain_copy(1, c).start()
 
-    gather_start(2)
+        gather_start(2 + c)
 
     @pl.when(jnp.logical_not(first))
     def _():
@@ -417,8 +423,10 @@
         swap_copy(2, other).start()
     pre_all[dp] = pre_t[pl.ds(pl.multiple_of(dp * pad, 16), pad), :]
 
+    gather_forward(2)
     gather_forward(1)
-    gather_forward(2)
+    for c in range(1, CHUNKS):
+        gather_forward(2 + c)
 
     @pl.when(jnp.logical_not(early))
     def _():
@@ -447,8 +455,9 @@
         def _():
             chain_copy(1, c).wait_send()
 
+    for i in range(len(gathered)):
+        gather_finish(i)
     for i in range(3):
-        gather_finish(i)
         for other in range(1, n_dp):
             swap_copy(i, other).wait()
     for other in range(1, n_code):
@@ -517,8 +526,8 @@
             dma((3,)),
             dma((2, CHUNKS)),
             dma((2, CHUNKS)),
-            dma((3, 2, chips)),
-            dma((3, 2, chips)),
+            dma((2 + CHUNKS, 2, chips)),
+            dma((2 + CHUNKS, 2, chips)),
             dma((3, n_dp)),
             dma((3, n_dp)),
             dma((n_code,)),

time: 192 us -> 193 us (level)
  no operation moved by 1% of the time
where the time goes in v4:
time: 193 us; the launch traced here: 191 us
  Pallas kernels  172 us (89%)
  matrix products  9.63 us (5%)
  local copies, waits for them, and re-layouts  5.36 us (3%)
  other arithmetic  3.16 us (2%)
    pallas_call x1, Pallas kernels, per_device(): pl.pallas_call(functools.partial(chain_kernel, n_dp, n_code), out_shape=o...  172 us
    dot_general x4, matrix products, over_rows(): lax.dot_general(left, right, (((0,), (0,)), ((), ())), preferred_element_...  9.63 us

profile of v4, /device:TPU:0, one launch (start us, length us, event | category | flops | bytes accessed | tf_op | source)
XLA Modules:
  0.0 191.3 jit_solution(8226834854738396272)
XLA Ops:
  0.6 0.0 copy-start
  0.6 0.0 copy-start.3
  0.7 1.6 copy-done
  2.2 0.7 convert_element_type.19
  2.9 0.7 and_bitcast_fusion
  3.6 0.0 copy-start.4
  3.6 0.9 gather_fusion
  4.4 1.8 bitcast_multiply_fusion
  6.3 0.0 copy-done.3
  6.3 0.8 pad.7.w1_own
  7.1 0.0 copy-done.4
  7.1 0.9 pad.8.w2_own
  8.0 0.0 copy-start.6
  8.0 172.5 %depth_chain.1 = (bf16[128,1024]{1,0:T(8,128)(2,1)}, bf16[8,128,512]{2,1,0:T(8,128)(2,1)}, bf16[8,128,1024]{2,1,0:T(8,128)(2,1)}, bf16[8,128,1024]{2,1,0:T(8,128...) custom-call(bf16[128,4096]{1,0:T(8,128)(2,1)} %temporal.1, ...), custom_call_target="tpu_custom_call" | custom-call | tf_op jit(solution)/shard_map/depth_chain/pallas_call | solution.py:501
  180.4 0.0 copy-start.8
  180.5 0.0 copy-done.6
  180.5 3.1 %fusion.5 = bf16[1,128,1024]{2,1,0:T(8,128)(2,1)} fusion(bf16[1024,1024]{1,0:T(8,128)(2,1)} %bitcast.51, s32[128]{0:T(128)S(1)} %iota_add_fusion, s32[1024]{0:T(1024)S(1)} %bitcast.55), kind=kOutput, calls=%fused_computation.10 | convolution fusion | flops 268697600 | bytes 2363904 | tf_op jit(solution)/shard_map/dot_general | solution.py:543
  183.6 0.0 copy-done.8
  183.6 0.0 copy-start.7
  183.6 0.0 copy-start.9
  183.6 2.7 %fusion.4 = bf16[1,1024,264]{1,2,0:T(8,128)(2,1)} fusion(bf16[8,128,1024]{2,1,0:T(8,128)(2,1)S(1)} %copy-done.8, bf16[8,272,128]{2,1,0:T(8,128)(2,1)} %get-tuple-element.16), kind=kOutput, calls=%fused_computation.8 | convolution fusion | flops 553918464 | bytes 3178496 | tf_op jit(solution)/shard_map/dot_general | solution.py:543
  186.3 0.0 copy-done.7
  186.3 0.0 copy-done.9
  186.3 0.0 copy-start.1
  186.3 0.0 copy-start.2
  186.3 1.5 fusion.3
  187.9 0.0 copy-done.1
  187.9 0.5 copy-done.2
  188.4 0.0 copy-start.5
  188.4 2.2 %fusion = bf16[1,512,1024]{2,1,0:T(8,128)(2,1)} fusion(bf16[8,128,512]{2,1,0:T(8,128)(2,1)S(1)} %copy-done.2, bf16[8,128,1024]{2,1,0:T(8,128)(2,1)S(1)} %copy-done.1), kind=kOutput, calls=%fused_computation.4 | convolution fusion | flops 1074266112 | bytes 4194304 | tf_op jit(solution)/shard_map/dot_general | solution.py:543
  190.6 0.0 copy-done.5
  190.6 0.7 copy.16
  (2 shorter events, 0.0 us)
Async XLA Ops:
  0.6 1.6 copy-start
  0.6 5.6 %copy-start.3 = (bf16[1,1024,264]{1,2,0:T(8,128)(2,1)S(1)}, bf16[1,1024,264]{1,2,0:T(8,128)(2,1)}, u32[]{:S(2)}) copy-start(bf16[1,1024,264]{1,2,0:T(8,128)(2,1)} %param.11) | copy-start | bytes 1622020
  3.6 3.6 %copy-start.4 = (bf16[1,1024,264]{1,2,0:T(8,128)(2,1)S(1)}, bf16[1,1024,264]{1,2,0:T(8,128)(2,1)}, u32[]{:S(2)}) copy-start(bf16[1,1024,264]{1,2,0:T(8,128)(2,1)} %param.12) | copy-start | bytes 1622020
  8.0 172.5 %copy-start.6 = (s32[1024,1]{0,1:T(1,128)S(1)}, s32[1024,1]{0,1:T(1,128)}, u32[]{:S(2)}) copy-start(s32[1024,1]{0,1:T(1,128)} %param.13) | copy-start | bytes 12292
  180.4 3.1 %copy-start.8 = (bf16[8,128,1024]{2,1,0:T(8,128)(2,1)S(1)}, bf16[8,128,1024]{2,1,0:T(8,128)(2,1)}, u32[]{:S(2)}) copy-start(bf16[8,128,1024]{2,1,0:T(8,128)(2,1)} %get-tuple-element.15) | copy-start | bytes 6291460
  183.6 2.7 %copy-start.7 = (bf16[8,128,1024]{2,1,0:T(8,128)(2,1)S(1)}, bf16[8,128,1024]{2,1,0:T(8,128)(2,1)}, u32[]{:S(2)}) copy-start(bf16[8,128,1024]{2,1,0:T(8,128)(2,1)} %get-tuple-element.17) | copy-start | bytes 6291460
  183.6 2.7 %copy-start.9 = (bf16[8,272,128]{2,1,0:T(8,128)(2,1)S(1)}, bf16[8,272,128]{2,1,0:T(8,128)(2,1)}, u32[]{:S(2)}) copy-start(bf16[8,272,128]{2,1,0:T(8,128)(2,1)} %get-tuple-element.18) | copy-start | bytes 1671172
  186.3 1.6 copy-start.1
  186.3 2.1 %copy-start.2 = (bf16[8,128,512]{2,1,0:T(8,128)(2,1)S(1)}, bf16[8,128,512]{2,1,0:T(8,128)(2,1)}, u32[]{:S(2)}) copy-start(bf16[8,128,512]{2,1,0:T(8,128)(2,1)} %get-tuple-element.13) | copy-start | bytes 3145732
  188.4 2.2 %copy-start.5 = (bf16[128,1024]{1,0:T(8,128)(2,1)S(1)}, bf16[128,1024]{1,0:T(8,128)(2,1)}, u32[]{:S(2)}) copy-start(bf16[128,1024]{1,0:T(8,128)(2,1)} %get-tuple-element.28) | copy-start | bytes 786436
